TPU v7x, 32 devices: a whole 2x2x4 slice. The times are simulated.
32 devices in a mesh: dp: 4 (over y, core), row: 2 (over x), col: 4 (over z).
Axes of the slice: x: 2, y: 2, z: 4, core: 2. Of those that a mesh axis runs over, the one named last changes fastest.
Arguments:
- inputs: bfloat16 [2048, 6144], P('dp', 'row'), may hold values from -600 to 600
- saved_qkv: bfloat16 [2048, 3, 3072], P('dp', None, 'col'), may hold values from -6 to 6
- saved_up: bfloat16 [2048, 12288], P('dp', 'col'), may hold values from -6 to 6
- cotangent: bfloat16 [2048, 6144], P('dp', 'row'), may hold values from -6 to 6
- weight_qkv: bfloat16 [6144, 3, 3072], P('row', None, 'col'), may hold values from -0.078125 to 0.078125
- weight_up: bfloat16 [6144, 12288], P('row', 'col'), may hold values from -0.078125 to 0.078125
- weight_attn: bfloat16 [3072, 6144], P('col', 'row'), may hold values from -0.109375 to 0.109375
- weight_down: bfloat16 [12288, 6144], P('col', 'row'), may hold values from -0.0546875 to 0.0546875
Outputs:
- grad_inputs: bfloat16 [2048, 6144], P(('dp', 'col'), 'row')
- grad_qkv: bfloat16 [2, 4, 768, 3, 3072], P('row', 'dp', None, None, 'col')
- grad_up: bfloat16 [2, 4, 768, 12288], P('row', 'dp', None, 'col')
- grad_attn: bfloat16 [4, 4, 192, 6144], P('col', 'dp', None, 'row')
- grad_down: bfloat16 [4, 4, 768, 6144], P('col', 'dp', None, 'row')
All inputs are finite; a program needn't handle non-finite values.
Results may differ from a plain program's by a relative error of at most 0.0039.
The roundings to bfloat16 on the way count: a program that leaves them out, or rounds other values in their place, can miss the bound.
Values may be sent and summed in bfloat16 or wider, within the bound.
No kernel may reach another device: no remote copies, remote signals or barrier semaphores. Data moves between devices by JAX's collectives and lax.ppermute only.
A program may use at most 192 MiB of HBM per device.

v0:
```python
import jax
import jax.numpy as jnp
from jax import lax
from jax.sharding import PartitionSpec as P

HD = 128
S = 256
EPS = 1e-06
SQRT_HALF = 0.7071067811865476
INV_ROOT_TWO_PI = 0.3989422804014327


def gelu_exact(values):
    return 0.5 * values * (1.0 + jax.scipy.special.erf(values * SQRT_HALF))


def gelu_slope(values):
    cumul = 0.5 * (1.0 + jax.scipy.special.erf(values * SQRT_HALF))
    return cumul + values * jnp.exp(-0.5 * values * values) * INV_ROOT_TWO_PI


def head_norm(values):
    average = jnp.mean(values, axis=-1, keepdims=True)
    centred = values - average
    inv_std = lax.rsqrt(jnp.mean(centred * centred, axis=-1, keepdims=True) + EPS)
    return (centred * inv_std, inv_std)


def head_norm_back(normed, inv_std, upstream):
    first = jnp.mean(upstream, axis=-1, keepdims=True)
    cross = jnp.mean(upstream * normed, axis=-1, keepdims=True)
    return inv_std * (upstream - first - normed * cross)


def body(inputs, saved_qkv, saved_up, cotangent, weight_qkv, weight_up, weight_attn, weight_down):
    f32 = jnp.float32
    bf16 = jnp.bfloat16
    tok_rows, feat_local = inputs.shape
    head_cols = saved_qkv.shape[2]
    up_cols = saved_up.shape[1]
    n_row = lax.axis_size("row")
    n_col = lax.axis_size("col")
    width = feat_local * n_row
    head_count = head_cols // HD
    images = tok_rows // S
    values = inputs.astype(f32)
    first_sum, square_sum = lax.psum(
        (jnp.sum(values, axis=1), jnp.sum(values * values, axis=1)), "row"
    )
    average = (first_sum / width)[:, None]
    inv_std = lax.rsqrt((square_sum / width)[:, None] - average * average + EPS)
    normed = (values - average) * inv_std
    normed_b = normed.astype(bf16)
    qkv5 = saved_qkv.reshape(images, S, 3, head_count, HD)
    query = qkv5[:, :, 0]
    keyed = qkv5[:, :, 1]
    valued = qkv5[:, :, 2]
    q_norm, q_inv = head_norm(query.astype(f32))
    k_norm, k_inv = head_norm(keyed.astype(f32))
    qn_b = q_norm.astype(bf16)
    kn_b = k_norm.astype(bf16)
    scale = HD ** (-0.5)
    scores = jnp.einsum("bqhd,bkhd->bhqk", qn_b, kn_b, preferred_element_type=f32) * scale
    expo = jnp.exp(scores)
    probs = expo / jnp.sum(expo, axis=-1, keepdims=True)
    probs_b = probs.astype(bf16)
    attended = jnp.einsum("bhqk,bkhd->bqhd", probs_b, valued, preferred_element_type=f32).astype(
        bf16
    )
    attended = attended.reshape(tok_rows, head_cols)
    hidden_b = gelu_exact(saved_up.astype(f32)).astype(bf16)
    part_attn = jnp.einsum("td,ad->ta", cotangent, weight_attn, preferred_element_type=f32)
    part_hidden = jnp.einsum("td,fd->tf", cotangent, weight_down, preferred_element_type=f32)
    sum_attn, sum_hidden = lax.psum((part_attn, part_hidden), "row")
    grad_o = sum_attn.astype(bf16)
    grad_pre = (sum_hidden * gelu_slope(saved_up.astype(f32))).astype(bf16)
    grad_o4 = grad_o.reshape(images, S, head_count, HD)
    grad_probs = jnp.einsum("bqhd,bkhd->bhqk", grad_o4, valued, preferred_element_type=f32)
    grad_value = jnp.einsum("bhqk,bqhd->bkhd", probs_b, grad_o4, preferred_element_type=f32).astype(
        bf16
    )
    rowdot = jnp.sum(probs * grad_probs, axis=-1, keepdims=True)
    grad_scores = (probs * (grad_probs - rowdot) * scale).astype(bf16)
    grad_qn = jnp.einsum("bhqk,bkhd->bqhd", grad_scores, kn_b, preferred_element_type=f32)
    grad_kn = jnp.einsum("bhqk,bqhd->bkhd", grad_scores, qn_b, preferred_element_type=f32)
    grad_query = head_norm_back(q_norm, q_inv, grad_qn).astype(bf16)
    grad_key = head_norm_back(k_norm, k_inv, grad_kn).astype(bf16)
    grad_flat = jnp.stack([grad_query, grad_key, grad_value], axis=2).reshape(
        tok_rows, 3 * head_cols
    )
    flat_weight = weight_qkv.reshape(feat_local, 3 * head_cols)
    share_rows = tok_rows // n_col
    total = jnp.einsum("ta,da->td", grad_flat, flat_weight, preferred_element_type=f32)
    grad_normed = lax.psum_scatter(
        total + jnp.einsum("tf,df->td", grad_pre, weight_up, preferred_element_type=f32),
        "col",
        scatter_dimension=0,
        tiled=True,
    )
    first_row = lax.axis_index("col") * share_rows
    normed_share = lax.dynamic_slice_in_dim(normed, first_row, share_rows, 0)
    inv_share = lax.dynamic_slice_in_dim(inv_std, first_row, share_rows, 0)
    cot_share = lax.dynamic_slice_in_dim(cotangent, first_row, share_rows, 0)
    sum_grad, sum_cross = lax.psum(
        (jnp.sum(grad_normed, axis=1), jnp.sum(grad_normed * normed_share, axis=1)), "row"
    )
    branch_term = (
        grad_normed - (sum_grad / width)[:, None] - normed_share * (sum_cross / width)[:, None]
    )
    grad_inputs = (cot_share.astype(f32) + inv_share * branch_term).astype(bf16)
    moved_normed, moved_attended, moved_hidden = (
        lax.all_to_all(normed_b, "dp", split_axis=1, concat_axis=0, tiled=True),
        lax.all_to_all(attended, "dp", split_axis=1, concat_axis=0, tiled=True),
        lax.all_to_all(hidden_b, "dp", split_axis=1, concat_axis=0, tiled=True),
    )
    cot_piece = lax.all_gather(cotangent, "dp", axis=0, tiled=True)
    flat_piece = lax.all_gather(grad_flat, "dp", axis=0, tiled=True)
    pre_piece = lax.all_gather(grad_pre, "dp", axis=0, tiled=True)
    new_qkv = jnp.einsum("td,ta->da", moved_normed, flat_piece, preferred_element_type=f32)
    new_up = jnp.einsum("td,tf->df", moved_normed, pre_piece, preferred_element_type=f32)
    new_attn = jnp.einsum("ta,td->ad", moved_attended, cot_piece, preferred_element_type=f32)
    new_down = jnp.einsum("tf,td->fd", moved_hidden, cot_piece, preferred_element_type=f32)
    grad_qkv = new_qkv.astype(bf16).reshape(1, 1, new_qkv.shape[0], 3, head_cols)
    grad_up = new_up.astype(bf16).reshape(1, 1, new_up.shape[0], up_cols)
    grad_attn = new_attn.astype(bf16).reshape(1, 1, new_attn.shape[0], feat_local)
    grad_down = new_down.astype(bf16).reshape(1, 1, new_down.shape[0], feat_local)
    return (grad_inputs, grad_qkv, grad_up, grad_attn, grad_down)


def solution(mesh):
    return jax.shard_map(
        body,
        mesh=mesh,
        in_specs=(
            P("dp", "row"),
            P("dp", None, "col"),
            P("dp", "col"),
            P("dp", "row"),
            P("row", None, "col"),
            P("row", "col"),
            P("col", "row"),
            P("col", "row"),
        ),
        out_specs=(
            P(("dp", "col"), "row"),
            P("row", "dp", None, None, "col"),
            P("row", "dp", None, "col"),
            P("col", "dp", None, "row"),
            P("col", "dp", None, "row"),
        ),
        check_vma=False,
    )
```

profile of v0, /device:TPU:0, one launch (start us, length us, event | category | flops | bytes accessed | tf_op | source)
XLA Modules:
  0.0 490.4 jit_solution(17388915969645549124)
XLA Ops:
  8.0 0.0 all-reduce.5.cloned.1.call-start
  8.0 16.4 %fusion.87 = f32[512,3072]{1,0:T(8,128)} fusion(bf16[512,3072]{1,0:T(8,128)(2,1)} %param.11, bf16[3072,3072]{1,0:T(8,128)(2,1)} %param.15), kind=kOutput, calls=%fused_computation.110 | convolution fusion | flops 9663676416 | bytes 28311552 | tf_op jit(solution)/shard_map/td,fd->tf/dot_general | solution.py:73
  24.5 0.0 all-gather.4.cloned.1.call-start
  24.5 7.2 %fusion.85 = f32[512,768]{1,0:T(8,128)} fusion(bf16[512,3072]{1,0:T(8,128)(2,1)} %param.11, bf16[768,3072]{1,0:T(8,128)(2,1)} %param.14), kind=kOutput, calls=%fused_computation.108 | convolution fusion | flops 2415919104 | bytes 9437184 | tf_op jit(solution)/shard_map/td,ad->ta/dot_general | solution.py:72
  31.7 1.0 convert_reduce_fusion
  32.7 79.4 %all-reduce.6 = (bf16[512,768]{1,0:T(8,128)(2,1)S(1)}, f32[512]{0:T(512)S(1)}, f32[512]{0:T(512)S(1)}) all-reduce(f32[512,768]{1,0:T(8,128)} %fusion.85, f32[512]{0:T(512)S(1)} %get-tuple-element.16, f32[512]{0:T(512)S(1)} %get-tuple-element.15), channel_id=1, replica_groups=mesh['dp'=4,'row'=2,'col'=4] {'row'}, use_global_device_ids=true, to_apply=%region_9.0 | all-reduce | flops 394240 | bytes 2367488 | tf_op jit(solution)/shard_map/psum | solution.py:74
  112.2 0.9 reshape.107
  113.1 0.6 copy.35
  113.7 2.8 copy.25
  116.5 2.1 reshape.99
  118.7 3.8 fusion.80
  122.4 2.5 copy.54
  124.9 0.2 convert_reduce_fusion.1
  125.1 0.2 fusion.47
  125.3 0.2 fusion.36
  125.6 2.2 fusion.55
  127.8 2.5 fusion.17
  130.4 7.8 %bitcast_reduce_fusion = (f32[2,256,6]{1,2,0:T(8,128)S(1)}, f32[2,256,6]{1,2,0:T(8,128)S(1)}, f32[2,6,128,256]{3,2,1,0:T(8,128)}) fusion(f32[2,256,6]{1,2,0:T(8,128)S(1)} %add_rsqrt_fusion, f32[2,256,6]{1,2,0:T(8,128)S(1)} %broadcast_multiply_fusion.4, bf16[2,256,1,6,128]{1,0,4,3,2:T(2,128)(2,1)S(1)} %get-tuple-element.34, f32[2,6,256,256]{2,3,1,0:T(8,128)} %fusion.55, ...), kind=kOutput, calls=%fused_computation.66 | convolution fusion | flops 212333824 | bytes 9523200 | tf_op jit(solution)/shard_map/bhqk,bqhd->bkhd/dot_general | solution.py:85
  138.2 7.7 %bitcast_reduce_fusion.1 = (f32[2,256,6]{1,2,0:T(8,128)S(1)}, f32[2,256,6]{1,2,0:T(8,128)S(1)}, f32[2,6,128,256]{3,2,1,0:T(8,128)}) fusion(f32[2,256,6]{1,2,0:T(8,128)S(1)} %add_rsqrt_fusion.1, f32[2,256,6]{1,2,0:T(8,128)S(1)} %broadcast_multiply_fusion.5, bf16[2,256,1,6,128]{1,0,4,3,2:T(2,128)(2,1)S(1)} %get-tuple-element.33, ...), kind=kOutput, calls=%fused_computation.68 | convolution fusion | flops 212333824 | bytes 9523200 | tf_op jit(solution)/shard_map/bhqk,bkhd->bqhd/dot_general | solution.py:84
  145.9 2.1 fusion.52
  148.1 0.1 copy-done.8
  148.2 0.4 fusion.53
  148.6 0.7 copy-done.10
  149.2 0.8 fusion.50
  150.0 0.3 pad_maximum_fusion
  150.3 2.4 copy.37
  152.7 1.9 copy.60
  154.6 0.0 all-gather.4.cloned.1.call-update
  154.6 0.0 reduce-scatter.2.cloned.1.call-start
  154.7 19.4 %copy.38 = bf16[3072,3,768]{0,2,1:T(8,128)(2,1)} copy(bf16[3072,3,768]{2,0,1:T(8,128)(2,1)} %param.12) | data formatting | bytes 28311552 | tf_op args[4]
  174.1 12.6 %fusion.86 = f32[512,3072]{1,0:T(8,128)} fusion(bf16[512,2304]{0,1:T(8,128)(2,1)S(1)} %bitcast.152, bf16[3072,2304]{0,1:T(8,128)(2,1)} %bitcast.147), kind=kOutput, calls=%fused_computation.109 | convolution fusion | flops 7247757312 | bytes 22806528 | tf_op jit(solution)/shard_map/ta,da->td/dot_general | solution.py:93
  186.7 27.9 %all-reduce.5.cloned.1.call-done = f32[512,3072]{1,0:T(8,128)} async-done(((f32[512,3072]{1,0:T(8,128)}), f32[512,3072]{1,0:T(8,128)}) %all-reduce.5.cloned.1.call-update) | async-done | bytes 6291472 | tf_op jit(solution)/shard_map/psum | solution.py:74
  214.6 7.8 %fusion.11 = (bf16[512,3072]{1,0:T(8,128)(2,1)}, bf16[512,3072]{1,0:T(8,128)(2,1)S(1)}) fusion(bf16[512,3072]{1,0:T(8,128)(2,1)} %param.10, f32[512,3072]{1,0:T(8,128)} %all-reduce.5.cloned.1.call-done), kind=kLoop, calls=%fused_computation.19 | loop fusion | flops 22020096 | bytes 15728640 | tf_op jit(solution)/shard_map/convert_element_type | solution.py:71
  222.4 17.5 %convolution_add_fusion = f32[512,3072]{1,0:T(8,128)} fusion(f32[512,3072]{1,0:T(8,128)} %fusion.86, bf16[512,3072]{1,0:T(8,128)(2,1)S(1)} %get-tuple-element.31, bf16[3072,3072]{1,0:T(8,128)(2,1)} %param.13), kind=kOutput, calls=%fused_computation.23 | convolution fusion | flops 9665249280 | bytes 34603008 | tf_op jit(solution)/shard_map/tf,df->td/dot_general | solution.py:95
  240.0 0.0 reduce-scatter.2.cloned.1.call-update
  240.0 0.0 all-gather.8.cloned.1.call-start
  240.1 0.5 all-gather.8.cloned.1.call-update
  240.6 0.0 all-gather.6.cloned.1.call-start
  240.6 0.5 all-gather.6.cloned.1.call-update
  241.2 3.6 fusion.51
  244.8 4.0 copy.42
  248.8 3.2 all_to_all.46
  252.0 4.7 all-to-all-start.1
  256.7 4.0 fusion.72
  260.7 1.9 copy.96
  262.6 14.6 %all-to-all-done.1 = bf16[512,4,192]{0,2,1:T(8,128)(2,1)} async-done(((bf16[512,4,192]{0,2,1:T(8,128)(2,1)}), bf16[512,4,192]{0,2,1:T(8,128)(2,1)}, u32[]{:S(2)}, u32[]{:S(2)}) %all-to-all-start.1) | async-done | bytes 786464 | tf_op jit(solution)/shard_map/all_to_all | solution.py:113
  277.2 4.9 %all-to-all-start = ((bf16[512,4,768]{2,0,1:T(8,128)(2,1)}), bf16[512,4,768]{2,0,1:T(8,128)(2,1)}, u32[]{:S(2)}, u32[]{:S(2)}) async-start(bf16[512,4,768]{2,0,1:T(8,128)(2,1)} %bitcast.146), calls=%async_computation.1 | async-start | bytes 6291456 | tf_op jit(solution)/shard_map/all_to_all | solution.py:112
  282.1 0.1 dynamic-slice.3
  282.2 2.1 copy.59
  284.3 1.9 copy.95
  286.2 67.0 %all-to-all-done = bf16[512,4,768]{2,0,1:T(8,128)(2,1)} async-done(((bf16[512,4,768]{2,0,1:T(8,128)(2,1)}), bf16[512,4,768]{2,0,1:T(8,128)(2,1)}, u32[]{:S(2)}, u32[]{:S(2)}) %all-to-all-start) | async-done | bytes 3145760 | tf_op jit(solution)/shard_map/all_to_all | solution.py:112
  353.2 4.7 all-to-all-start.2
  357.9 0.0 all-gather.4.cloned.1.call-done
  357.9 13.2 %convolution_convert_fusion.2 = bf16[768,2304]{1,0:T(8,128)(2,1)} fusion(bf16[2048,768]{1,0:T(8,128)(2,1)} %bitcast.11, bf16[2048,2304]{0,1:T(8,128)(2,1)} %all-gather.4.cloned.1.call-done), kind=kOutput, calls=%fused_computation.22 | convolution fusion | flops 7249526784 | bytes 16121856 | tf_op jit(solution)/shard_map/td,ta->da/dot_general | solution.py:119
  371.1 4.5 copy.40
  375.6 3.7 copy.45
  379.3 2.7 fusion.79
  382.1 5.1 %all-reduce = (f32[128]{0:T(128)S(1)}, f32[128]{0:T(128)S(1)}) all-reduce(f32[128]{0:T(128)S(1)} %get-tuple-element.18, f32[128]{0:T(128)S(1)} %get-tuple-element.17), channel_id=1, replica_groups=mesh['dp'=4,'row'=2,'col'=4] {'row'}, use_global_device_ids=true, to_apply=%region_20.0 | all-reduce | flops 256 | bytes 2048 | tf_op jit(solution)/shard_map/psum | solution.py:104
  387.2 3.2 add_convert_fusion
  390.4 8.2 %fusion.14 = bf16[1,1,192,3072]{3,2,1,0:T(8,128)(2,1)} fusion(bf16[2048,192]{0,1:T(8,128)(2,1)S(1)} %bitcast.154, bf16[2048,3072]{1,0:T(8,128)(2,1)} %all-gather.8.cloned.1.call-done), kind=kOutput, calls=%fused_computation.27 | convolution fusion | flops 2416508928 | bytes 14548992 | tf_op jit(solution)/shard_map/ta,td->ad/dot_general | solution.py:121
  398.6 11.4 %all-to-all-done.2 = bf16[512,4,768]{2,0,1:T(8,128)(2,1)} async-done(((bf16[512,4,768]{2,0,1:T(8,128)(2,1)}), bf16[512,4,768]{2,0,1:T(8,128)(2,1)}, u32[]{:S(2)}, u32[]{:S(2)}) %all-to-all-start.2) | async-done | bytes 3145760 | tf_op jit(solution)/shard_map/all_to_all | solution.py:114
  410.0 15.5 %fusion.13 = bf16[1,1,768,3072]{3,2,1,0:T(8,128)(2,1)} fusion(bf16[2048,768]{1,0:T(8,128)(2,1)} %bitcast.19, bf16[2048,3072]{1,0:T(8,128)(2,1)} %all-gather.8.cloned.1.call-done), kind=kOutput, calls=%fused_computation.25 | convolution fusion | flops 9666035712 | bytes 20447232 | tf_op jit(solution)/shard_map/tf,td->fd/dot_general | solution.py:122
  425.5 41.8 %all-gather.6.cloned.1.call-done = bf16[2048,3072]{1,0:T(8,128)(2,1)} async-done(((bf16[512,3072]{1,0:T(8,128)(2,1)}), bf16[2048,3072]{1,0:T(8,128)(2,1)}) %all-gather.6.cloned.1.call-update) | async-done | bytes 12582928 | tf_op jit(solution)/shard_map/all_gather | solution.py:118
  467.3 15.3 %fusion.12 = bf16[1,1,768,3072]{3,2,1,0:T(8,128)(2,1)} fusion(bf16[2048,768]{1,0:T(8,128)(2,1)} %bitcast.11, bf16[2048,3072]{1,0:T(8,128)(2,1)} %all-gather.6.cloned.1.call-done), kind=kOutput, calls=%fused_computation.24 | convolution fusion | flops 9666035712 | bytes 20447232 | tf_op jit(solution)/shard_map/td,tf->df/dot_general | solution.py:120
  (34 shorter events, 0.1 us)
Async XLA Ops:
  8.0 206.6 %all-reduce.5.cloned.1.call-start = ((), (), s32[]{:S(2)}) async-start(), calls=%async_computation.4 | async-start | bytes 12582912 | tf_op jit(solution)/shard_map/psum | solution.py:74
  24.4 7.3 %copy-start = (bf16[512,3072]{1,0:T(8,128)(2,1)S(1)}, bf16[512,3072]{1,0:T(8,128)(2,1)}, u32[]{:S(2)}) copy-start(bf16[512,3072]{1,0:T(8,128)(2,1)} %param.8) | copy-start | bytes 9437188
  24.5 333.5 %all-gather.4.cloned.1.call-start = ((), (), s32[]{:S(2)}) async-start(), calls=%async_computation.6 | async-start | bytes 11796480 | tf_op jit(solution)/shard_map/all_gather | solution.py:117
  124.9 2.9 copy-start.6
  145.9 2.2 copy-start.8
  145.9 3.3 copy-start.10
  154.6 19.5 %copy-start.4 = (bf16[288,8,2,256]{3,1,2,0:T(8,128)(2,1)S(1)}, bf16[288,8,2,256]{3,1,2,0:T(8,128)(2,1)}, u32[]{:S(2)}) copy-start(bf16[288,8,2,256]{3,1,2,0:T(8,128)(2,1)} %copy.60) | copy-start | bytes 7077892
  154.6 224.7 %reduce-scatter.2.cloned.1.call-start = ((), (), s32[]{:S(2)}) async-start(), calls=%async_computation.5 | async-start | bytes 7864320 | tf_op jit(solution)/shard_map/reduce_scatter | solution.py:94
  222.4 17.5 %copy-start.2 = (bf16[512,3072]{1,0:T(8,128)(2,1)}, bf16[512,3072]{1,0:T(8,128)(2,1)S(1)}, u32[]{:S(2)}) copy-start(bf16[512,3072]{1,0:T(8,128)(2,1)S(1)} %get-tuple-element.31) | copy-start | bytes 9437188
  240.0 1.2 copy-start.7
  240.0 150.4 %all-gather.8.cloned.1.call-start = ((), (), s32[]{:S(2)}) async-start(), calls=%async_computation.8 | async-start | bytes 15728640 | tf_op jit(solution)/shard_map/all_gather | solution.py:116
  240.6 226.7 %all-gather.6.cloned.1.call-start = ((), (), s32[]{:S(2)}) async-start(), calls=%async_computation.7 | async-start | bytes 15728640 | tf_op jit(solution)/shard_map/all_gather | solution.py:118
  244.8 11.9 %copy-start.1 = (bf16[512,3072]{1,0:T(8,128)(2,1)S(1)}, bf16[512,3072]{1,0:T(8,128)(2,1)}, u32[]{:S(2)}) copy-start(bf16[512,3072]{1,0:T(8,128)(2,1)} %param.8) | copy-start | bytes 9437188
  252.0 25.2 %all-to-all-start.1 = ((bf16[512,4,192]{0,2,1:T(8,128)(2,1)}), bf16[512,4,192]{0,2,1:T(8,128)(2,1)}, u32[]{:S(2)}, u32[]{:S(2)}) async-start(bf16[512,4,192]{0,2,1:T(8,128)(2,1)} %all_to_all.46), calls=%async_computation.2 | async-start | bytes 1572864 | tf_op jit(solution)/shard_map/all_to_all | solution.py:113
  277.2 7.1 %copy-start.3 = (bf16[512,3072]{1,0:T(8,128)(2,1)S(1)}, bf16[512,3072]{1,0:T(8,128)(2,1)}, u32[]{:S(2)}) copy-start(bf16[512,3072]{1,0:T(8,128)(2,1)} %get-tuple-element.30) | copy-start | bytes 9437188
  277.2 76.0 %all-to-all-start = ((bf16[512,4,768]{2,0,1:T(8,128)(2,1)}), bf16[512,4,768]{2,0,1:T(8,128)(2,1)}, u32[]{:S(2)}, u32[]{:S(2)}) async-start(bf16[512,4,768]{2,0,1:T(8,128)(2,1)} %bitcast.146), calls=%async_computation.1 | async-start | bytes 6291456 | tf_op jit(solution)/shard_map/all_to_all | solution.py:112
  353.2 56.7 %all-to-all-start.2 = ((bf16[512,4,768]{2,0,1:T(8,128)(2,1)}), bf16[512,4,768]{2,0,1:T(8,128)(2,1)}, u32[]{:S(2)}, u32[]{:S(2)}) async-start(bf16[512,4,768]{2,0,1:T(8,128)(2,1)} %bitcast.145), calls=%async_computation.3 | async-start | bytes 6291456 | tf_op jit(solution)/shard_map/all_to_all | solution.py:114
  379.3 7.8 %copy-start.5 = (f32[128,3072]{1,0:T(8,128)S(1)}, f32[128,3072]{1,0:T(8,128)}, u32[]{:S(2)}) copy-start(f32[128,3072]{1,0:T(8,128)} %reduce-scatter.2.cloned.1.call-done) | copy-start | bytes 4718596
  382.1 8.3 %copy-start.9 = (bf16[4,24,8,512]{3,2,0,1:T(8,128)(2,1)S(1)}, bf16[4,24,8,512]{3,2,0,1:T(8,128)(2,1)}, u32[]{:S(2)}) copy-start(bf16[4,24,8,512]{3,2,0,1:T(8,128)(2,1)} %copy.59) | copy-start | bytes 2359300
Sparse Core Ops, SparseCore 0:
  24.6 190.0 all-reduce.4
  240.1 110.7 reduce-scatter.1
Sparse Core Ops, SparseCore 1:
  154.7 64.6 all-gather.3
  242.0 127.3 all-gather.7
  371.4 95.8 all-gather.5
where the time goes:
time: 499 us; the launch traced here: 490 us
  waiting for transfers between devices  164 us (33%)
  matrix products  131 us (26%)
  blocking collectives  84.5 us (17%)
  local copies, waits for them, and re-layouts  58.4 us (12%)
  other arithmetic  22.3 us (4%)
  between operations  16.1 us (3%)
  starting transfers between devices  14.5 us (3%)
    psum x1, blocking collectives, body(): sum_attn, sum_hidden = lax.psum((part_attn, part_hidden), 'row')  79.4 us
    all_to_all x1, waiting for transfers between devices, body(): lax.all_to_all(normed_b, 'dp', split_axis=1, concat_axis=0, tiled=True)  67 us
    all_gather x1, waiting for transfers between devices, body(): pre_piece = lax.all_gather(grad_pre, 'dp', axis=0, tiled=True)  41.8 us
    unnamed x27, local copies, waits for them, and re-layouts  31 us
    psum x1, waiting for transfers between devices, body(): sum_attn, sum_hidden = lax.psum((part_attn, part_hidden), 'row')  27.9 us
    dot_general x1, matrix products, body(): jnp.einsum('tf,df->td', grad_pre, weight_up, preferred_element_type=f32)  17.5 us
    dot_general x1, matrix products, body(): jnp.einsum('td,fd->tf', cotangent, weight_down, preferred_element_type=f32)  16.4 us
    dot_general x1, matrix products, body(): jnp.einsum('tf,td->fd', moved_hidden, cot_piece, preferred_element_type=f32)  15.5 us
  transfers between devices with their start and end apart: 8, of which 5 were waited for; matrix products, arithmetic and copies ran while one was open for 36% of the time, Pallas kernels for 0%

commit v1 on v0

--- a/solution.py
+++ b/solution.py
@@ -115,9 +115,39 @@
     )
     cot_piece = lax.all_gather(cotangent, "dp", axis=0, tiled=True)
     flat_piece = lax.all_gather(grad_flat, "dp", axis=0, tiled=True)
-    pre_piece = lax.all_gather(grad_pre, "dp", axis=0, tiled=True)
     new_qkv = jnp.einsum("td,ta->da", moved_normed, flat_piece, preferred_element_type=f32)
-    new_up = jnp.einsum("td,tf->df", moved_normed, pre_piece, preferred_element_type=f32)
+    size, here, extent = (lax.axis_size("dp"), lax.axis_index("dp"), grad_pre.shape[0])
+    upward = [(i, (i + 1) % size) for i in range(size)]
+    left = [(i, (i - 1) % size) for i in range(size)]
+    middle = size // 2
+    from_left = from_right = grad_pre
+    total_2 = jnp.einsum(
+        "td,tf->df",
+        lax.dynamic_slice_in_dim(moved_normed, here * extent, grad_pre.shape[0], axis=0),
+        grad_pre,
+        preferred_element_type=f32,
+    )
+    for turn in range(1, middle + 1):
+        from_left = lax.ppermute(from_left, "dp", upward)
+        if turn < size - middle:
+            from_right = lax.ppermute(from_right, "dp", left)
+            total_2 = total_2 + jnp.einsum(
+                "td,tf->df",
+                lax.dynamic_slice_in_dim(
+                    moved_normed, (here + turn) % size * extent, from_right.shape[0], axis=0
+                ),
+                from_right,
+                preferred_element_type=f32,
+            )
+        total_2 = total_2 + jnp.einsum(
+            "td,tf->df",
+            lax.dynamic_slice_in_dim(
+                moved_normed, (here - turn) % size * extent, from_left.shape[0], axis=0
+            ),
+            from_left,
+            preferred_element_type=f32,
+        )
+    new_up = total_2
     new_attn = jnp.einsum("ta,td->ad", moved_attended, cot_piece, preferred_element_type=f32)
     new_down = jnp.einsum("tf,td->fd", moved_hidden, cot_piece, preferred_element_type=f32)
     grad_qkv = new_qkv.astype(bf16).reshape(1, 1, new_qkv.shape[0], 3, head_cols)

time: 499 us -> 551 us (1.10)
  matrix products: 131 us -> 157 us
  waiting for transfers between devices: 164 us -> 179 us
  starting transfers between devices: 14.5 us -> 24.1 us
    all_to_all x1, waiting for transfers between devices: 14.6 us -> 71.6 us  [body(): lax.all_to_all(attended, 'dp', split_axis=1, concat_axis=0, tiled=True)]
    ppermute x0 -> x3, waiting for transfers between devices: none -> 45.2 us  [the longest x1 45.1 us: body(): from_right = lax.ppermute(from_right, 'dp', left)]
    all_gather x1 -> x0, waiting for transfers between devices: 41.8 us -> none  [body(): pre_piece = lax.all_gather(grad_pre, 'dp', axis=0, tiled=True)]
    all_to_all x1, waiting for transfers between devices: 67 us -> 34.2 us  [body(): lax.all_to_all(normed_b, 'dp', split_axis=1, concat_axis=0, tiled=True)]
    dot_general x1 -> x4, matrix products: 15.3 us -> 41 us  [the longest x2 24.2 us: body(): jnp.einsum('td,tf->df', lax.dynamic_slice_in_dim(moved_normed, (here - tu...]
    all_to_all x1, waiting for transfers between devices: 11.4 us -> 0.01 us  [body(): lax.all_to_all(hidden_b, 'dp', split_axis=1, concat_axis=0, tiled=True)]
    all_to_all x1, starting transfers between devices: 4.93 us -> 11.4 us  [body(): lax.all_to_all(normed_b, 'dp', split_axis=1, concat_axis=0, tiled=True)]
    unnamed x27 -> x25, local copies, waits for them, and re-layouts: 31 us -> 31.5 us
  transfers between devices with their start and end apart: 8 -> 10, of which waited for: 5 -> 4; matrix products, arithmetic and copies ran while one was open for 36% -> 37% of each run, Pallas kernels for 0% -> 0%
where the time goes in v1:
time: 551 us; the launch traced here: 542 us
  waiting for transfers between devices  179 us (32%)
  matrix products  157 us (28%)
  blocking collectives  84.4 us (15%)
  local copies, waits for them, and re-layouts  58.9 us (11%)
  starting transfers between devices  24.1 us (4%)
  other arithmetic  22.6 us (4%)
  between operations  16.2 us (3%)
    psum x1, blocking collectives, body(): sum_attn, sum_hidden = lax.psum((part_attn, part_hidden), 'row')  79.4 us
    all_to_all x1, waiting for transfers between devices, body(): lax.all_to_all(attended, 'dp', split_axis=1, concat_axis=0, tiled=True)  71.6 us
    ppermute x1, waiting for transfers between devices, body(): from_right = lax.ppermute(from_right, 'dp', left)  45.1 us
    all_to_all x1, waiting for transfers between devices, body(): lax.all_to_all(normed_b, 'dp', split_axis=1, concat_axis=0, tiled=True)  34.2 us
    unnamed x25, local copies, waits for them, and re-layouts  31.5 us
    psum x1, waiting for transfers between devices, body(): sum_attn, sum_hidden = lax.psum((part_attn, part_hidden), 'row')  27.8 us
    dot_general x2, matrix products, body(): jnp.einsum('td,tf->df', lax.dynamic_slice_in_dim(moved_normed, (here - tu...  24.2 us
    dot_general x1, matrix products, body(): jnp.einsum('tf,df->td', grad_pre, weight_up, preferred_element_type=f32)  17.3 us
  transfers between devices with their start and end apart: 10, of which 4 were waited for; matrix products, arithmetic and copies ran while one was open for 37% of the time, Pallas kernels for 0%

profile of v1, /device:TPU:0, one launch (start us, length us, event | category | flops | bytes accessed | tf_op | source)
XLA Modules:
  0.0 542.1 jit_solution(18093880154042535752)
XLA Ops:
  8.0 0.0 all-reduce.5.cloned.1.call-start
  8.0 16.4 %fusion.98 = f32[512,3072]{1,0:T(8,128)} fusion(bf16[512,3072]{1,0:T(8,128)(2,1)} %param.11, bf16[3072,3072]{1,0:T(8,128)(2,1)} %param.15), kind=kOutput, calls=%fused_computation.121 | convolution fusion | flops 9663676416 | bytes 28311552 | tf_op jit(solution)/shard_map/td,fd->tf/dot_general | solution.py:73
  24.5 0.0 all-gather.3.cloned.1.call-start
  24.5 7.2 %fusion.96 = f32[512,768]{1,0:T(8,128)} fusion(bf16[512,3072]{1,0:T(8,128)(2,1)} %param.11, bf16[768,3072]{1,0:T(8,128)(2,1)} %param.14), kind=kOutput, calls=%fused_computation.119 | convolution fusion | flops 2415919104 | bytes 9437184 | tf_op jit(solution)/shard_map/td,ad->ta/dot_general | solution.py:72
  31.7 1.0 convert_reduce_fusion
  32.7 79.4 %all-reduce.6 = (bf16[512,768]{1,0:T(8,128)(2,1)S(1)}, f32[512]{0:T(512)S(1)}, f32[512]{0:T(512)S(1)}) all-reduce(f32[512,768]{1,0:T(8,128)} %fusion.96, f32[512]{0:T(512)S(1)} %get-tuple-element.16, f32[512]{0:T(512)S(1)} %get-tuple-element.15), channel_id=1, replica_groups=mesh['dp'=4,'row'=2,'col'=4] {'row'}, use_global_device_ids=true, to_apply=%region_9.0 | all-reduce | flops 394240 | bytes 2367488 | tf_op jit(solution)/shard_map/psum | solution.py:74
  112.2 0.9 reshape.107
  113.1 0.6 copy.35
  113.7 2.8 copy.25
  116.5 2.1 reshape.99
  118.7 3.8 fusion.91
  122.4 2.5 copy.54
  125.0 0.2 convert_reduce_fusion.1
  125.1 0.2 fusion.47
  125.4 0.2 fusion.36
  125.6 2.2 fusion.55
  127.9 2.5 fusion.17
  130.4 7.8 %bitcast_reduce_fusion = (f32[2,256,6]{1,2,0:T(8,128)S(1)}, f32[2,256,6]{1,2,0:T(8,128)S(1)}, f32[2,6,128,256]{3,2,1,0:T(8,128)}) fusion(f32[2,256,6]{1,2,0:T(8,128)S(1)} %add_rsqrt_fusion, f32[2,256,6]{1,2,0:T(8,128)S(1)} %broadcast_multiply_fusion.4, bf16[2,256,1,6,128]{1,0,4,3,2:T(2,128)(2,1)S(1)} %get-tuple-element.34, f32[2,6,256,256]{2,3,1,0:T(8,128)} %fusion.55, ...), kind=kOutput, calls=%fused_computation.66 | convolution fusion | flops 212333824 | bytes 9523200 | tf_op jit(solution)/shard_map/bhqk,bqhd->bkhd/dot_general | solution.py:85
  138.3 7.7 %bitcast_reduce_fusion.1 = (f32[2,256,6]{1,2,0:T(8,128)S(1)}, f32[2,256,6]{1,2,0:T(8,128)S(1)}, f32[2,6,128,256]{3,2,1,0:T(8,128)}) fusion(f32[2,256,6]{1,2,0:T(8,128)S(1)} %add_rsqrt_fusion.1, f32[2,256,6]{1,2,0:T(8,128)S(1)} %broadcast_multiply_fusion.5, bf16[2,256,1,6,128]{1,0,4,3,2:T(2,128)(2,1)S(1)} %get-tuple-element.33, ...), kind=kOutput, calls=%fused_computation.68 | convolution fusion | flops 212333824 | bytes 9523200 | tf_op jit(solution)/shard_map/bhqk,bkhd->bqhd/dot_general | solution.py:84
  146.0 2.2 fusion.52
  148.2 0.0 copy-done.7
  148.2 0.4 fusion.53
  148.6 0.6 copy-done.9
  149.3 0.8 fusion.50
  150.0 0.3 pad_maximum_fusion
  150.3 2.4 copy.37
  152.8 1.9 copy.60
  154.7 0.0 reduce-scatter.2.cloned.1.call-start
  154.7 19.4 %copy.38 = bf16[3072,3,768]{0,2,1:T(8,128)(2,1)} copy(bf16[3072,3,768]{2,0,1:T(8,128)(2,1)} %param.12) | data formatting | bytes 28311552 | tf_op args[4]
  174.1 12.7 %fusion.97 = f32[512,3072]{1,0:T(8,128)} fusion(bf16[512,2304]{0,1:T(8,128)(2,1)S(1)} %bitcast.154, bf16[3072,2304]{0,1:T(8,128)(2,1)} %bitcast.149), kind=kOutput, calls=%fused_computation.120 | convolution fusion | flops 7247757312 | bytes 22806528 | tf_op jit(solution)/shard_map/ta,da->td/dot_general | solution.py:93
  186.8 27.8 %all-reduce.5.cloned.1.call-done = f32[512,3072]{1,0:T(8,128)} async-done(((f32[512,3072]{1,0:T(8,128)}), f32[512,3072]{1,0:T(8,128)}) %all-reduce.5.cloned.1.call-update) | async-done | bytes 6291472 | tf_op jit(solution)/shard_map/psum | solution.py:74
  214.6 8.9 %fusion.11 = (bf16[512,3072]{1,0:T(8,128)(2,1)}, bf16[512,3072]{1,0:T(8,128)(2,1)}) fusion(bf16[512,3072]{1,0:T(8,128)(2,1)} %param.10, f32[512,3072]{1,0:T(8,128)} %all-reduce.5.cloned.1.call-done), kind=kLoop, calls=%fused_computation.20 | loop fusion | flops 22020096 | bytes 15728640 | tf_op jit(solution)/shard_map/convert_element_type | solution.py:71
  223.5 17.3 %convolution_add_fusion = f32[512,3072]{1,0:T(8,128)} fusion(f32[512,3072]{1,0:T(8,128)} %fusion.97, bf16[512,3072]{1,0:T(8,128)(2,1)} %get-tuple-element.31, bf16[3072,3072]{1,0:T(8,128)(2,1)} %param.13), kind=kOutput, calls=%fused_computation.23 | convolution fusion | flops 9665249280 | bytes 34603008 | tf_op jit(solution)/shard_map/tf,df->td/dot_general | solution.py:95
  240.9 0.0 all-gather.5.cloned.1.call-start
  240.9 0.5 all-gather.5.cloned.1.call-update
  241.4 0.1 collective-permute-start.1
  241.5 0.5 copy-done.6
  242.0 3.6 fusion.51
  245.6 3.9 copy.42
  249.5 3.2 all_to_all.46
  252.7 4.5 all-to-all-start.1
  257.2 4.0 fusion.83
  261.2 1.9 copy.96
  263.1 71.6 %all-to-all-done.1 = bf16[512,4,192]{0,2,1:T(8,128)(2,1)} async-done(((bf16[512,4,192]{0,2,1:T(8,128)(2,1)}), bf16[512,4,192]{0,2,1:T(8,128)(2,1)}, u32[]{:S(2)}, u32[]{:S(2)}) %all-to-all-start.1) | async-done | bytes 786464 | tf_op jit(solution)/shard_map/all_to_all | solution.py:113
  334.6 11.4 %all-to-all-start = ((bf16[512,4,768]{2,0,1:T(8,128)(2,1)}), bf16[512,4,768]{2,0,1:T(8,128)(2,1)}, u32[]{:S(2)}, u32[]{:S(2)}) async-start(bf16[512,4,768]{2,0,1:T(8,128)(2,1)} %bitcast.148), calls=%async_computation.1 | async-start | bytes 6291456 | tf_op jit(solution)/shard_map/all_to_all | solution.py:112
  346.0 3.4 collective-permute-start
  349.5 0.1 dynamic-slice.3
  349.5 2.1 copy.59
  351.6 1.9 copy.95
  353.5 34.2 %all-to-all-done = bf16[512,4,768]{2,0,1:T(8,128)(2,1)} async-done(((bf16[512,4,768]{2,0,1:T(8,128)(2,1)}), bf16[512,4,768]{2,0,1:T(8,128)(2,1)}, u32[]{:S(2)}, u32[]{:S(2)}) %all-to-all-start) | async-done | bytes 3145760 | tf_op jit(solution)/shard_map/all_to_all | solution.py:112
  387.8 4.7 all-to-all-start.2
  392.4 8.4 %fusion.62 = f32[768,3072]{1,0:T(8,128)} fusion(bf16[512,3072]{1,0:T(8,128)(2,1)} %get-tuple-element.31, bf16[2048,768]{1,0:T(8,128)(2,1)} %bitcast.11, s32[]{:T(128)S(6)} %select_n.33), kind=kOutput, calls=%fused_computation.87 | convolution fusion | flops 2415919104 | bytes 13369348 | tf_op jit(solution)/shard_map/td,tf->df/dot_general | solution.py:124
  400.8 8.4 %fusion.58 = f32[768,3072]{1,0:T(8,128)} fusion(bf16[512,3072]{1,0:T(8,128)(2,1)} %collective-permute-done.1, bf16[2048,768]{1,0:T(8,128)(2,1)} %bitcast.11, s32[]{:T(128)S(6)} %select_n.37), kind=kOutput, calls=%fused_computation.83 | convolution fusion | flops 2415919104 | bytes 13369348 | tf_op jit(solution)/shard_map/td,tf->df/dot_general | solution.py:142
  409.1 45.1 %collective-permute-done = bf16[512,3072]{1,0:T(8,128)(2,1)} collective-permute-done((bf16[512,3072]{1,0:T(8,128)(2,1)}, bf16[512,3072]{1,0:T(8,128)(2,1)}, u32[]{:S(2)}, u32[]{:S(2)}) %collective-permute-start) | collective-permute-done | bytes 3145760 | tf_op jit(solution)/shard_map/ppermute | solution.py:133
  454.3 8.4 %fusion.60 = f32[768,3072]{1,0:T(8,128)} fusion(bf16[512,3072]{1,0:T(8,128)(2,1)} %collective-permute-done, bf16[2048,768]{1,0:T(8,128)(2,1)} %bitcast.11, s32[]{:T(128)S(6)} %select_n.35), kind=kOutput, calls=%fused_computation.85 | convolution fusion | flops 2415919104 | bytes 13369348 | tf_op jit(solution)/shard_map/td,tf->df/dot_general | solution.py:134
  462.7 15.9 %fusion.13 = bf16[1,1,768,3072]{3,2,1,0:T(8,128)(2,1)} fusion(bf16[512,3072]{1,0:T(8,128)(2,1)} %collective-permute-done.2, f32[768,3072]{1,0:T(8,128)} %fusion.58, f32[768,3072]{1,0:T(8,128)} %fusion.62, f32[768,3072]{1,0:T(8,128)} %fusion.60, bf16[2048,768]{1,0:T(8,128)(2,1)} %bitcast.11, s32[]{:T(128)S(6)} %select_n.39), kind=kOutput, calls=%fused_computation.25 | convolution fusion | flops 2425356288 | bytes 36962308 | tf_op jit(solution)/shard_map/td,tf->df/dot_general | solution.py:142
  478.6 13.4 %convolution_convert_fusion.1 = bf16[768,2304]{1,0:T(8,128)(2,1)} fusion(bf16[2048,768]{1,0:T(8,128)(2,1)} %bitcast.11, bf16[2048,2304]{0,1:T(8,128)(2,1)} %all-gather.3.cloned.1.call-done), kind=kOutput, calls=%fused_computation.22 | convolution fusion | flops 7249526784 | bytes 16121856 | tf_op jit(solution)/shard_map/td,ta->da/dot_general | solution.py:118
  491.9 4.5 copy.40
  496.5 3.7 copy.45
  500.1 2.2 fusion.90
  502.3 5.0 all-reduce
  507.3 8.2 %fusion.14 = bf16[1,1,192,3072]{3,2,1,0:T(8,128)(2,1)} fusion(bf16[2048,192]{0,1:T(8,128)(2,1)S(1)} %bitcast.156, bf16[2048,3072]{1,0:T(8,128)(2,1)} %all-gather.5.cloned.1.call-done), kind=kOutput, calls=%fused_computation.27 | convolution fusion | flops 2416508928 | bytes 14548992 | tf_op jit(solution)/shard_map/ta,td->ad/dot_general | solution.py:151
  515.5 15.7 %fusion.12 = bf16[1,1,768,3072]{3,2,1,0:T(8,128)(2,1)} fusion(bf16[2048,768]{1,0:T(8,128)(2,1)} %bitcast.19, bf16[2048,3072]{1,0:T(8,128)(2,1)} %all-gather.5.cloned.1.call-done), kind=kOutput, calls=%fused_computation.24 | convolution fusion | flops 9666035712 | bytes 20447232 | tf_op jit(solution)/shard_map/tf,td->fd/dot_general | solution.py:152
  531.2 3.0 add_convert_fusion.1
  (38 shorter events, 0.2 us)
Async XLA Ops:
  8.0 206.6 %all-reduce.5.cloned.1.call-start = ((), (), s32[]{:S(2)}) async-start(), calls=%async_computation.4 | async-start | bytes 12582912 | tf_op jit(solution)/shard_map/psum | solution.py:74
  24.4 7.3 %copy-start = (bf16[512,3072]{1,0:T(8,128)(2,1)S(1)}, bf16[512,3072]{1,0:T(8,128)(2,1)}, u32[]{:S(2)}) copy-start(bf16[512,3072]{1,0:T(8,128)(2,1)} %param.8) | copy-start | bytes 9437188
  24.5 454.1 %all-gather.3.cloned.1.call-start = ((), (), s32[]{:S(2)}) async-start(), calls=%async_computation.6 | async-start | bytes 11796480 | tf_op jit(solution)/shard_map/all_gather | solution.py:117
  124.9 2.9 copy-start.5
  146.0 2.2 copy-start.7
  146.0 3.3 copy-start.9
  154.7 19.5 %copy-start.3 = (bf16[288,8,2,256]{3,1,2,0:T(8,128)(2,1)S(1)}, bf16[288,8,2,256]{3,1,2,0:T(8,128)(2,1)}, u32[]{:S(2)}) copy-start(bf16[288,8,2,256]{3,1,2,0:T(8,128)(2,1)} %copy.60) | copy-start | bytes 7077892
  154.7 345.5 %reduce-scatter.2.cloned.1.call-start = ((), (), s32[]{:S(2)}) async-start(), calls=%async_computation.5 | async-start | bytes 7864320 | tf_op jit(solution)/shard_map/reduce_scatter | solution.py:94
  240.8 1.1 copy-start.6
  240.9 266.5 %all-gather.5.cloned.1.call-start = ((), (), s32[]{:S(2)}) async-start(), calls=%async_computation.7 | async-start | bytes 15728640 | tf_op jit(solution)/shard_map/all_gather | solution.py:116
  241.4 108.0 %collective-permute-start.1 = (bf16[512,3072]{1,0:T(8,128)(2,1)}, bf16[512,3072]{1,0:T(8,128)(2,1)}, u32[]{:S(2)}, u32[]{:S(2)}) collective-permute-start(bf16[512,3072]{1,0:T(8,128)(2,1)} %get-tuple-element.31), channel_id=1, source_target_pairs={{0,8},{8,16},{16,24},{24,0},{1,9},{9,17},{17,25},{25,1},{2,10},{10... | collective-permute-start | bytes 9437192 | tf_op jit(solution)/shard_map/ppermute | solution.py:131
  245.6 11.6 %copy-start.1 = (bf16[512,3072]{1,0:T(8,128)(2,1)S(1)}, bf16[512,3072]{1,0:T(8,128)(2,1)}, u32[]{:S(2)}) copy-start(bf16[512,3072]{1,0:T(8,128)(2,1)} %param.8) | copy-start | bytes 9437188
  252.7 81.9 %all-to-all-start.1 = ((bf16[512,4,192]{0,2,1:T(8,128)(2,1)}), bf16[512,4,192]{0,2,1:T(8,128)(2,1)}, u32[]{:S(2)}, u32[]{:S(2)}) async-start(bf16[512,4,192]{0,2,1:T(8,128)(2,1)} %all_to_all.46), calls=%async_computation.2 | async-start | bytes 1572864 | tf_op jit(solution)/shard_map/all_to_all | solution.py:113
  334.6 17.0 %copy-start.2 = (bf16[512,3072]{1,0:T(8,128)(2,1)S(1)}, bf16[512,3072]{1,0:T(8,128)(2,1)}, u32[]{:S(2)}) copy-start(bf16[512,3072]{1,0:T(8,128)(2,1)} %get-tuple-element.30) | copy-start | bytes 9437188
  334.6 53.1 %all-to-all-start = ((bf16[512,4,768]{2,0,1:T(8,128)(2,1)}), bf16[512,4,768]{2,0,1:T(8,128)(2,1)}, u32[]{:S(2)}, u32[]{:S(2)}) async-start(bf16[512,4,768]{2,0,1:T(8,128)(2,1)} %bitcast.148), calls=%async_computation.1 | async-start | bytes 6291456 | tf_op jit(solution)/shard_map/all_to_all | solution.py:112
  346.0 108.3 %collective-permute-start = (bf16[512,3072]{1,0:T(8,128)(2,1)}, bf16[512,3072]{1,0:T(8,128)(2,1)}, u32[]{:S(2)}, u32[]{:S(2)}) collective-permute-start(bf16[512,3072]{1,0:T(8,128)(2,1)} %get-tuple-element.31), channel_id=1, source_target_pairs={{0,24},{8,0},{16,8},{24,16},{1,25},{9,1},{17,9},{25,17},{2,26},{10... | collective-permute-start | bytes 9437192 | tf_op jit(solution)/shard_map/ppermute | solution.py:133
  349.4 113.3 %collective-permute-start.2 = (bf16[512,3072]{1,0:T(8,128)(2,1)}, bf16[512,3072]{1,0:T(8,128)(2,1)}, u32[]{:S(2)}, u32[]{:S(2)}) collective-permute-start(bf16[512,3072]{1,0:T(8,128)(2,1)} %collective-permute-done.1), channel_id=1, source_target_pairs={{0,8},{8,16},{16,24},{24,0},{1,9},{9,17},{17,25},{25,1},{2,10},{10... | collective-permute-start | bytes 9437192 | tf_op jit(solution)/shard_map/ppermute | solution.py:131
  387.8 127.8 %all-to-all-start.2 = ((bf16[512,4,768]{2,0,1:T(8,128)(2,1)}), bf16[512,4,768]{2,0,1:T(8,128)(2,1)}, u32[]{:S(2)}, u32[]{:S(2)}) async-start(bf16[512,4,768]{2,0,1:T(8,128)(2,1)} %bitcast.147), calls=%async_computation.3 | async-start | bytes 6291456 | tf_op jit(solution)/shard_map/all_to_all | solution.py:114
  500.1 7.2 %copy-start.8 = (bf16[4,24,8,512]{3,2,0,1:T(8,128)(2,1)S(1)}, bf16[4,24,8,512]{3,2,0,1:T(8,128)(2,1)}, u32[]{:S(2)}) copy-start(bf16[4,24,8,512]{3,2,0,1:T(8,128)(2,1)} %copy.59) | copy-start | bytes 2359300
  515.5 15.7 %copy-start.4 = (f32[128,3072]{1,0:T(8,128)S(1)}, f32[128,3072]{1,0:T(8,128)}, u32[]{:S(2)}) copy-start(f32[128,3072]{1,0:T(8,128)} %reduce-scatter.2.cloned.1.call-done) | copy-start | bytes 4718596
Sparse Core Ops, SparseCore 0:
  24.6 190.0 all-reduce.4
  241.0 110.7 reduce-scatter.1
Sparse Core Ops, SparseCore 1:
  154.7 64.6 all-gather.2
  242.9 117.4 all-gather.4
